TPU v7x, 32 devices: a whole 2x2x4 slice. The times are simulated.
32 devices in a mesh: row: 8 (over y, x, core), col: 4 (over z).
Axes of the slice: x: 2, y: 2, z: 4, core: 2. Of those that a mesh axis runs over, the one named last changes fastest.
Arguments:
- skew_matrix: float32 [16384, 16384], P('row', 'col'), may hold values from -80 to 80, as said below
- first_reflector: float32 [16384, 128], P('row'), may hold values from -0.05625 to 0.05625
- first_factor: float32 [128, 128], replicated, may hold values from -0.6 to 1.5, as said below
- second_reflector: float32 [16384, 128], P('row'), may hold values from -0.05625 to 0.05625
- second_factor: float32 [128, 128], replicated, may hold values from -0.6 to 1.5, as said below
- vectors: float32 [16384, 4096], P('row', 'col'), may hold values from -6 to 6
Outputs:
- updated_matrix: float32 [16384, 16384], P('row', 'col')
- back_vectors: float32 [16384, 4096], P('row', 'col')
Inputs may be any that keep to these rules, and one draw needn't show every extreme that they name: skew_matrix is skew-symmetric: entry (i, j) equals minus entry (j, i) exactly. first_factor is upper triangular with a positive diagonal. second_factor is upper triangular with a positive diagonal.
All inputs are finite; a program needn't handle non-finite values.
Results may differ from a plain program's by a relative error of at most 0.000059.
Values sent between devices are 32-bit elements; how exact they have to be, the bound alone decides.
A program may use at most 192 MiB of HBM per device.

v0:
```python
import jax
import jax.numpy as jnp
from jax import lax
from jax.sharding import PartitionSpec as P


def multiply(left, right):
    return jnp.dot(left, right, precision=lax.Precision.HIGHEST, preferred_element_type=jnp.float32)


def inner_rows(left, right):
    return lax.dot_general(
        left,
        right,
        (((0,), (0,)), ((), ())),
        precision=lax.Precision.HIGHEST,
        preferred_element_type=jnp.float32,
    )


def transform(matrix, own_rows, col_rows, factor):
    partial_rows = multiply(matrix, col_rows)
    summed_rows = lax.psum(partial_rows, "col")
    partial_cols = inner_rows(matrix, own_rows)
    summed_cols = lax.psum(partial_cols, "row")
    plain_cols = -summed_cols
    gram = lax.psum(inner_rows(own_rows, summed_rows), "row")
    correction = multiply(multiply(factor.T, gram), factor)
    fixed_rows = multiply(summed_rows, factor) - 0.5 * multiply(own_rows, correction)
    fixed_cols = multiply(plain_cols, factor) - 0.5 * multiply(col_rows, correction)
    left = jnp.concatenate([own_rows, -fixed_rows], axis=1)
    right = jnp.concatenate([fixed_cols, col_rows], axis=1)
    update = lax.dot_general(
        left,
        right,
        (((1,), (1,)), ((), ())),
        precision=lax.Precision.HIGHEST,
        preferred_element_type=jnp.float32,
    )
    return matrix + update


def shards(skew_matrix, first_reflector, first_factor, second_reflector, second_factor, vectors):
    joined = jnp.concatenate([first_reflector, second_reflector], axis=1)
    correlation, projected = lax.psum(
        (inner_rows(first_reflector, second_reflector), inner_rows(joined, vectors)), "row"
    )
    top_right = -multiply(multiply(first_factor, correlation), second_factor)
    zeros_block = jnp.zeros_like(second_factor)
    compact = jnp.concatenate(
        [
            jnp.concatenate([first_factor, top_right], axis=1),
            jnp.concatenate([zeros_block, second_factor], axis=1),
        ],
        axis=0,
    )
    back_vectors = vectors - multiply(joined, multiply(compact, projected))
    cols_here = skew_matrix.shape[1]
    col_index = lax.axis_index("col")
    whole_first, whole_second = (
        lax.all_gather(first_reflector, "row", axis=0, tiled=True),
        lax.all_gather(second_reflector, "row", axis=0, tiled=True),
    )
    col_start = col_index * cols_here
    panel_first = lax.dynamic_slice_in_dim(whole_first, col_start, cols_here, 0)
    panel_second = lax.dynamic_slice_in_dim(whole_second, col_start, cols_here, 0)
    inner = transform(skew_matrix, first_reflector, panel_first, first_factor)
    updated_matrix = transform(inner, second_reflector, panel_second, second_factor)
    return (updated_matrix, back_vectors)


def solution(mesh):
    in_specs = (P("row", "col"), P("row", None), P(), P("row", None), P(), P("row", "col"))
    out_specs = (P("row", "col"), P("row", "col"))
    return jax.shard_map(shards, mesh=mesh, in_specs=in_specs, out_specs=out_specs, check_vma=False)
```

profile of v0, /device:TPU:0, one launch (start us, length us, event | category | flops | bytes accessed | tf_op | source)
XLA Modules:
  0.0 549.0 jit_solution(17140156105039725318)
XLA Ops:
  7.2 0.0 all-gather.3.cloned.1.call-start
  7.2 0.7 all-gather.3.cloned.1.call-update
  7.9 0.0 all-reduce.8.cloned.1.call-start
  7.9 58.9 %all-gather.3.cloned.1.call-done = f32[16384,128]{1,0:T(8,128)} async-done(((f32[2048,128]{1,0:T(8,128)}), f32[16384,128]{1,0:T(8,128)}) %all-gather.3.cloned.1.call-update) | async-done | bytes 8388624 | tf_op jit(solution)/shard_map/all_gather | solution.py:61
  66.9 1.7 constant_dynamic-slice_fusion.1
  68.6 1.3 copy-done.4
  69.9 41.9 %convolution_bitcast_fusion = f32[2048,128]{0,1:T(8,128)} fusion(f32[4096,128]{1,0:T(8,128)S(1)} %constant_dynamic-slice_fusion.1, f32[2048,4096]{1,0:T(8,128)} %param.6), kind=kOutput, calls=%fused_computation.13 | convolution fusion | flops 12884901888 | bytes 36700160 | tf_op jit(solution)/shard_map/dot_general | solution.py:8
  111.8 0.0 all-reduce.8.cloned.1.call-update
  111.8 0.0 all-gather.5.cloned.1.call-start
  111.9 0.7 all-gather.5.cloned.1.call-update
  112.6 0.0 all-reduce.14.cloned.1.call-start
  112.6 0.4 copy-done
  113.0 1.1 constant_dynamic-update-slice_fusion.1
  114.1 1.1 constant_dynamic-update-slice_fusion
  115.2 57.1 %fusion.39 = f32[4096,128]{1,0:T(8,128)} fusion(f32[2048,4096]{1,0:T(8,128)} %param.6, f32[2048,128]{1,0:T(8,128)S(1)} %copy-done), kind=kOutput, calls=%fused_computation.56 | convolution fusion | flops 12884901888 | bytes 36700160 | tf_op jit(solution)/shard_map/dot_general | solution.py:12
  172.3 0.0 all-reduce.8.cloned.1.call-done
  172.3 3.1 convolution_bitcast_fusion.2
  175.4 0.0 all-reduce.10.cloned.1.call-start
  175.5 11.1 %fusion.47 = f32[256,1024]{1,0:T(8,128)} fusion(f32[2048,256]{1,0:T(8,128)} %constant_dynamic-update-slice_fusion, f32[2048,1024]{1,0:T(8,128)} %param.11), kind=kOutput, calls=%fused_computation.64 | convolution fusion | flops 6442450944 | bytes 11534336 | tf_op jit(solution)/shard_map/dot_general | solution.py:12
  186.5 2.4 fusion.45
  189.0 30.4 %all-gather.5.cloned.1.call-done = f32[16384,128]{1,0:T(8,128)} async-done(((f32[2048,128]{1,0:T(8,128)}), f32[16384,128]{1,0:T(8,128)}) %all-gather.5.cloned.1.call-update) | async-done | bytes 8388624 | tf_op jit(solution)/shard_map/all_gather | solution.py:62
  219.3 3.2 constant_dynamic-slice_fusion
  222.6 1.8 fusion.36
  224.4 60.9 %all-reduce.14.cloned.1.call-done = (f32[4096,128]{1,0:T(8,128)}, f32[128,128]{0,1:T(8,128)}) async-done(((f32[4096,128]{1,0:T(8,128)}, f32[128,128]{0,1:T(8,128)}), (f32[4096,128]{1,0:T(8,128)}, f32[128,128]{0,1:T(8,128)})) %all-reduce.14.cloned.1.call-update) | async-done | bytes 2162704 | tf_op jit(solution)/shard_map/psum | solution.py:25
  285.3 3.6 fusion.22
  288.9 0.2 fusion.37
  289.1 0.3 fusion.38
  289.4 1.9 fusion.1
  291.3 1.0 fusion.13
  292.3 33.7 %convolution_add_fusion.1 = f32[2048,4096]{1,0:T(8,128)} fusion(f32[2048,4096]{1,0:T(8,128)} %param.6, f32[4096,128]{1,0:T(8,128)S(1)} %copy-done.5, f32[4096,128]{1,0:T(8,128)S(1)} %fusion.1, f32[2048,128]{1,0:T(8,128)S(1)} %fusion.13, f32[2048,128]{1,0:T(8,128)S(1)} %copy-done), kind=kOutput, calls=%fused_computation.1 | convolution fusion | flops 25779765248 | bytes 73400320 | tf_op jit(solution)/shard_map/dot_general | solution.py:33
  325.9 30.9 %fusion.40 = f32[2048,128]{1,0:T(8,128)} fusion(f32[2048,4096]{1,0:T(8,128)} %convolution_add_fusion.1, f32[4096,128]{1,0:T(8,128)S(1)} %copy-done.2), kind=kOutput, calls=%fused_computation.57 | convolution fusion | flops 12884901888 | bytes 36700160 | tf_op jit(solution)/shard_map/dot_general | solution.py:8
  356.8 0.0 all-reduce.12.cloned.1.call-start
  356.9 57.1 %fusion.44 = f32[4096,128]{1,0:T(8,128)} fusion(f32[2048,4096]{1,0:T(8,128)} %convolution_add_fusion.1, f32[2048,128]{1,0:T(8,128)S(1)} %copy-done.1), kind=kOutput, calls=%fused_computation.61 | convolution fusion | flops 12884901888 | bytes 36700160 | tf_op jit(solution)/shard_map/dot_general | solution.py:12
  414.0 0.0 all-reduce.10.cloned.1.call-done
  414.0 3.7 convolution_bitcast_fusion.1
  417.7 1.2 copy-done.7
  418.9 1.0 fusion.41
  419.9 68.0 %all-reduce.12.cloned.1.call-done = (f32[4096,128]{1,0:T(8,128)}, f32[128,128]{0,1:T(8,128)}, f32[256,1024]{1,0:T(8,128)}, f32[128,128]{1,0:T(8,128)}) async-done(((f32[4096,128]{1,0:T(8,128)}, f32[128,128]{0,1:T(8,128)}, f32[256,1024]{1,0:T(8,128)}, f32[128,128]{1,0:T(8,128)}), (f32[4096,128]{1,0:T(8,128)}, f32[128,128]{0,1:T(8,128)}, f32[256,1024]{1,0:T(8,128)}, ...) | async-done | bytes 3276816 | tf_op jit(solution)/shard_map/psum | solution.py:25
  487.9 3.6 fusion.20
  491.5 0.2 fusion.42
  491.7 0.3 fusion.43
  492.0 1.9 fusion
  493.9 1.0 fusion.10
  494.9 0.3 fusion.46
  495.2 0.3 convolution_negate_fusion
  495.5 1.0 fusion.24
  496.5 12.2 %convolution_subtract_fusion = f32[2048,1024]{1,0:T(8,128)} fusion(f32[2048,1024]{1,0:T(8,128)} %param.11, f32[2048,256]{1,0:T(8,128)} %constant_dynamic-update-slice_fusion, f32[256,1024]{1,0:T(8,128)S(1)} %fusion.24), kind=kOutput, calls=%fused_computation.6 | convolution fusion | flops 6444548096 | bytes 19922944 | tf_op jit(solution)/shard_map/dot_general | solution.py:8
  508.7 33.0 %convolution_add_fusion = f32[2048,4096]{1,0:T(8,128)} fusion(f32[2048,4096]{1,0:T(8,128)} %convolution_add_fusion.1, f32[4096,128]{1,0:T(8,128)S(1)} %copy-done.3, f32[4096,128]{1,0:T(8,128)S(1)} %fusion, f32[2048,128]{1,0:T(8,128)S(1)} %fusion.10, f32[2048,128]{1,0:T(8,128)S(1)} %copy-done.1), kind=kOutput, calls=%fused_computation | convolution fusion | flops 25779765248 | bytes 73400320 | tf_op jit(solution)/shard_map/dot_general | solution.py:33
  (28 shorter events, 0.1 us)
Async XLA Ops:
  7.2 59.7 %all-gather.3.cloned.1.call-start = ((), (), s32[]{:S(2)}) async-start(), calls=%async_computation | async-start | bytes 9437184 | tf_op jit(solution)/shard_map/all_gather | solution.py:61
  7.9 164.4 %all-reduce.8.cloned.1.call-start = ((), (), s32[]{:S(2)}) async-start(), calls=%async_computation.1 | async-start | bytes 2097152 | tf_op jit(solution)/shard_map/psum | solution.py:23
  68.6 1.3 copy-start.4
  111.8 1.2 copy-start
  111.8 2.3 copy-start.1
  111.8 107.5 %all-gather.5.cloned.1.call-start = ((), (), s32[]{:S(2)}) async-start(), calls=%async_computation.2 | async-start | bytes 9437184 | tf_op jit(solution)/shard_map/all_gather | solution.py:62
  112.6 172.7 %all-reduce.14.cloned.1.call-start = ((), (), s32[]{:S(2)}) async-start(), calls=%async_computation.5 | async-start | bytes 4325376 | tf_op jit(solution)/shard_map/psum | solution.py:25
  175.4 238.6 %all-reduce.10.cloned.1.call-start = ((), (), s32[]{:S(2)}) async-start(), calls=%async_computation.3 | async-start | bytes 2097152 | tf_op jit(solution)/shard_map/psum | solution.py:23
  189.0 33.6 %copy-start.8 = (f32[128,128]{1,0:T(8,128)S(1)}, f32[128,128]{1,0:T(8,128)}, u32[]{:S(2)}) copy-start(f32[128,128]{1,0:T(8,128)} %param.8) | copy-start | bytes 196612
  219.3 3.2 copy-start.6
  285.3 3.6 copy-start.12
  285.3 4.1 copy-start.5
  292.3 33.7 %copy-start.2 = (f32[4096,128]{1,0:T(8,128)S(1)}, f32[4096,128]{1,0:T(8,128)}, u32[]{:S(2)}) copy-start(f32[4096,128]{1,0:T(8,128)} %constant_dynamic-slice_fusion) | copy-start | bytes 6291460
  356.8 131.0 %all-reduce.12.cloned.1.call-start = ((), (), s32[]{:S(2)}) async-start(), calls=%async_computation.4 | async-start | bytes 6553600 | tf_op jit(solution)/shard_map/psum | solution.py:25
  417.7 1.2 copy-start.7
  417.7 1.2 copy-start.9
  487.9 3.6 copy-start.13
  487.9 4.1 copy-start.3
  493.8 1.0 copy-start.11
  493.9 1.6 copy-start.10
Sparse Core Ops, SparseCore 0:
  9.9 56.9 all-gather.2
  112.0 51.8 all-reduce.7
  165.8 53.5 all-gather.4
  223.1 62.1 all-reduce.13
  357.0 51.0 all-reduce.9
  417.8 70.0 all-reduce.11
where the time goes:
time: 559 us; the launch traced here: 549 us
  matrix products  304 us (54%)
  waiting for transfers between devices  220 us (39%)
  between operations  14.8 us (3%)
  local copies, waits for them, and re-layouts  10 us (2%)
    dot_general x6, matrix products, inner_rows(): lax.dot_general(left, right, (((0,), (0,)), ((), ())), precision=lax.Prec...  134 us
    psum x2, waiting for transfers between devices, transform(): summed_cols = lax.psum(partial_cols, 'row')  129 us
    dot_general x18, matrix products, multiply(): jnp.dot(left, right, precision=lax.Precision.HIGHEST, preferred_element_t...  103 us
    dot_general x2, matrix products, transform(): lax.dot_general(left, right, (((1,), (1,)), ((), ())), precision=lax.Prec...  66.7 us
    all_gather x1, waiting for transfers between devices, shards(): lax.all_gather(first_reflector, 'row', axis=0, tiled=True)  58.9 us
    all_gather x1, waiting for transfers between devices, shards(): lax.all_gather(second_reflector, 'row', axis=0, tiled=True)  30.4 us
  transfers between devices with their start and end apart: 6, of which 4 were waited for; matrix products, arithmetic and copies ran while one was open for 25% of the time, Pallas kernels for 0%

commit v1 on v0

--- a/solution.py
+++ b/solution.py
@@ -1,7 +1,27 @@
+import functools
 import jax
 import jax.numpy as jnp
 from jax import lax
 from jax.sharding import PartitionSpec as P
+
+
+def end_the_figure(frame, ax_name):
+    g_now = lax.axis_size(ax_name)
+    fresh = lax.axis_index(ax_name)
+    arr_out, b_next, odd = (g_now, fresh, frame.shape[0])
+    lower, mat_out = (frame, 1)
+    while mat_out < arr_out:
+        side_arr = range(arr_out)
+        view_out = map(lambda m: (m, (m - mat_out) % arr_out), side_arr)
+        y1 = list(view_out)
+        low = lax.ppermute(lower, axis_name=ax_name, perm=y1)
+        lower = jnp.concatenate([lower, low], 0)
+        mat_out = 2 * mat_out
+    q_next = jnp.roll(lower, b_next * odd, 0)
+    return q_next
+
+
+connect_the_plate = functools.partial(end_the_figure, ax_name="row")
 
 
 def multiply(left, right):
@@ -59,7 +79,7 @@
     col_index = lax.axis_index("col")
     whole_first, whole_second = (
         lax.all_gather(first_reflector, "row", axis=0, tiled=True),
-        lax.all_gather(second_reflector, "row", axis=0, tiled=True),
+        connect_the_plate(second_reflector),
     )
     col_start = col_index * cols_here
     panel_first = lax.dynamic_slice_in_dim(whole_first, col_start, cols_here, 0)

time: 559 us -> 579 us (1.036)
  local copies, waits for them, and re-layouts: 10 us -> 28.1 us
  other arithmetic: 0 us -> 6.55 us
    ppermute x0 -> x3, waiting for transfers between devices: none -> 59.2 us  [end_the_figure(): low = lax.ppermute(lower, axis_name=ax_name, perm=y1)]
    all_gather x1, waiting for transfers between devices: 58.9 us -> 0.01 us  [shards(): lax.all_gather(first_reflector, 'row', axis=0, tiled=True)]
    psum x2, waiting for transfers between devices: 0.04 us -> 36.9 us  [transform(): summed_rows = lax.psum(partial_rows, 'col')]
    all_gather x1 -> x0, waiting for transfers between devices: 30.4 us -> none  [shards(): lax.all_gather(second_reflector, 'row', axis=0, tiled=True)]
    unnamed x29 -> x37, local copies, waits for them, and re-layouts: 4.03 us -> 16.2 us
    psum x2, waiting for transfers between devices: 129 us -> 120 us  [transform(): summed_cols = lax.psum(partial_cols, 'row')]
    concatenate x0 -> x2, other arithmetic: none -> 6.55 us  [end_the_figure(): lower = jnp.concatenate([lower, low], 0)]
  transfers between devices with their start and end apart: 6 -> 8, of which waited for: 4 -> 6; matrix products, arithmetic and copies ran while one was open for 25% -> 36% of each run, Pallas kernels for 0% -> 0%
where the time goes in v1:
time: 579 us; the launch traced here: 573 us
  matrix products  303 us (52%)
  waiting for transfers between devices  217 us (37%)
  local copies, waits for them, and re-layouts  28.1 us (5%)
  between operations  14.3 us (2%)
  other arithmetic  6.55 us (1%)
    dot_general x6, matrix products, inner_rows(): lax.dot_general(left, right, (((0,), (0,)), ((), ())), precision=lax.Prec...  134 us
    psum x2, waiting for transfers between devices, transform(): summed_cols = lax.psum(partial_cols, 'row')  120 us
    dot_general x18, matrix products, multiply(): jnp.dot(left, right, precision=lax.Precision.HIGHEST, preferred_element_t...  103 us
    dot_general x2, matrix products, transform(): lax.dot_general(left, right, (((1,), (1,)), ((), ())), precision=lax.Prec...  66.6 us
    ppermute x3, waiting for transfers between devices, end_the_figure(): low = lax.ppermute(lower, axis_name=ax_name, perm=y1)  59.2 us
    psum x2, waiting for transfers between devices, transform(): summed_rows = lax.psum(partial_rows, 'col')  36.9 us
    unnamed x37, local copies, waits for them, and re-layouts  16.2 us
  transfers between devices with their start and end apart: 8, of which 6 were waited for; matrix products, arithmetic and copies ran while one was open for 36% of the time, Pallas kernels for 0%

profile of v1, /device:TPU:0, one launch (start us, length us, event | category | flops | bytes accessed | tf_op | source)
XLA Modules:
  0.0 573.0 jit_solution(2641443353003448031)
XLA Ops:
  7.2 0.7 all-gather.2.cloned.1.call-update
  8.0 3.4 collective-permute-start
  11.4 18.5 %collective-permute-done = f32[2048,128]{1,0:T(8,128)S(1)} collective-permute-done((f32[2048,128]{1,0:T(8,128)}, f32[2048,128]{1,0:T(8,128)S(1)}, u32[]{:S(2)}, u32[]{:S(2)}) %collective-permute-start) | collective-permute-done | bytes 1048608 | tf_op jit(solution)/shard_map/ppermute | solution.py:17
  29.9 2.7 pad_maximum_fusion.1
  32.7 1.1 copy-done
  33.8 1.1 constant_dynamic-update-slice_fusion.8
  34.9 2.4 fusion.45
  37.3 10.3 %fusion.47 = f32[256,1024]{1,0:T(8,128)} fusion(f32[2048,256]{1,0:T(8,128)S(1)} %get-tuple-element.8, f32[2048,1024]{1,0:T(8,128)} %param.11), kind=kOutput, calls=%fused_computation.74 | convolution fusion | flops 6442450944 | bytes 11534336 | tf_op jit(solution)/shard_map/dot_general | solution.py:32
  47.7 32.6 %collective-permute-done.1 = f32[4096,128]{1,0:T(8,128)} collective-permute-done((f32[4096,128]{1,0:T(8,128)}, f32[4096,128]{1,0:T(8,128)}, u32[]{:S(2)}, u32[]{:S(2)}) %collective-permute-start.1) | collective-permute-done | bytes 2097184 | tf_op jit(solution)/shard_map/ppermute | solution.py:17
  80.2 3.9 pad_maximum_fusion
  84.1 0.6 collective-permute-start.2
  84.7 56.9 %fusion.39 = f32[4096,128]{1,0:T(8,128)} fusion(f32[2048,4096]{1,0:T(8,128)} %param.6, f32[2048,128]{1,0:T(8,128)S(1)} %copy-done.1), kind=kOutput, calls=%fused_computation.66 | convolution fusion | flops 12884901888 | bytes 36700160 | tf_op jit(solution)/shard_map/dot_general | solution.py:32
  141.6 1.0 constant_dynamic-update-slice_fusion.6
  142.6 3.0 constant_dynamic-update-slice_fusion.5
  145.7 3.0 constant_dynamic-slice_fusion.1
  148.7 42.6 %convolution_bitcast_fusion = f32[2048,128]{0,1:T(8,128)} fusion(f32[4096,128]{1,0:T(8,128)} %constant_dynamic-slice_fusion.1, f32[2048,4096]{1,0:T(8,128)} %param.6), kind=kOutput, calls=%fused_computation.14 | convolution fusion | flops 12884901888 | bytes 36700160 | tf_op jit(solution)/shard_map/dot_general | solution.py:28
  191.4 8.1 %collective-permute-done.2 = f32[8192,128]{1,0:T(8,128)} collective-permute-done((f32[8192,128]{1,0:T(8,128)}, f32[8192,128]{1,0:T(8,128)}, u32[]{:S(2)}, u32[]{:S(2)}) %collective-permute-start.2) | collective-permute-done | bytes 4194336 | tf_op jit(solution)/shard_map/ppermute | solution.py:17
  199.5 4.5 constant_dynamic-update-slice_fusion.4
  204.0 1.0 constant_dynamic-update-slice_fusion.3
  205.0 1.0 constant_dynamic-update-slice_fusion.2
  206.0 3.1 constant_dynamic-update-slice_fusion.1
  209.1 36.9 %all-reduce.8.cloned.1.call-done = f32[2048,128]{0,1:T(8,128)} async-done(((f32[2048,128]{0,1:T(8,128)}), f32[2048,128]{0,1:T(8,128)}) %all-reduce.8.cloned.1.call-update) | async-done | bytes 1048592 | tf_op jit(solution)/shard_map/psum | solution.py:43
  246.0 3.0 convolution_bitcast_fusion.2
  249.0 4.5 constant_dynamic-update-slice_fusion
  253.5 3.3 constant_dynamic-slice_fusion
  256.8 1.8 fusion.36
  258.6 52.2 %all-reduce.14.cloned.1.call-done = (f32[4096,128]{1,0:T(8,128)}, f32[128,128]{0,1:T(8,128)}) async-done(((f32[4096,128]{1,0:T(8,128)}, f32[128,128]{0,1:T(8,128)}), (f32[4096,128]{1,0:T(8,128)}, f32[128,128]{0,1:T(8,128)})) %all-reduce.14.cloned.1.call-update) | async-done | bytes 2162704 | tf_op jit(solution)/shard_map/psum | solution.py:45
  310.8 3.6 fusion.22
  314.3 0.2 fusion.37
  314.6 0.3 fusion.38
  314.9 1.9 fusion.1
  316.7 1.0 fusion.13
  317.7 33.4 %convolution_add_fusion.1 = f32[2048,4096]{1,0:T(8,128)} fusion(f32[2048,4096]{1,0:T(8,128)} %param.6, f32[4096,128]{1,0:T(8,128)S(1)} %copy-done.4, f32[4096,128]{1,0:T(8,128)S(1)} %fusion.1, f32[2048,128]{1,0:T(8,128)S(1)} %fusion.13, f32[2048,128]{1,0:T(8,128)S(1)} %copy-done.1), kind=kOutput, calls=%fused_computation.1 | convolution fusion | flops 25779765248 | bytes 73400320 | tf_op jit(solution)/shard_map/dot_general | solution.py:53
  351.1 30.9 %fusion.40 = f32[2048,128]{1,0:T(8,128)} fusion(f32[2048,4096]{1,0:T(8,128)} %convolution_add_fusion.1, f32[4096,128]{1,0:T(8,128)S(1)} %copy-done.2), kind=kOutput, calls=%fused_computation.67 | convolution fusion | flops 12884901888 | bytes 36700160 | tf_op jit(solution)/shard_map/dot_general | solution.py:28
  382.1 57.3 %fusion.44 = f32[4096,128]{1,0:T(8,128)} fusion(f32[2048,4096]{1,0:T(8,128)} %convolution_add_fusion.1, f32[2048,128]{1,0:T(8,128)S(1)} %copy-done), kind=kOutput, calls=%fused_computation.71 | convolution fusion | flops 12884901888 | bytes 36700160 | tf_op jit(solution)/shard_map/dot_general | solution.py:32
  439.5 3.7 convolution_bitcast_fusion.1
  443.2 1.2 copy-done.8
  444.4 1.0 fusion.41
  445.3 68.0 %all-reduce.12.cloned.1.call-done = (f32[4096,128]{1,0:T(8,128)}, f32[128,128]{0,1:T(8,128)}, f32[256,1024]{1,0:T(8,128)}, f32[128,128]{1,0:T(8,128)}) async-done(((f32[4096,128]{1,0:T(8,128)}, f32[128,128]{0,1:T(8,128)}, f32[256,1024]{1,0:T(8,128)}, f32[128,128]{1,0:T(8,128)}), (f32[4096,128]{1,0:T(8,128)}, f32[128,128]{0,1:T(8,128)}, f32[256,1024]{1,0:T(8,128)}, ...) | async-done | bytes 3276816 | tf_op jit(solution)/shard_map/psum | solution.py:45
  513.3 3.6 fusion.20
  517.2 0.3 fusion.43
  517.5 1.9 fusion
  519.4 1.0 fusion.10
  520.4 0.3 fusion.46
  520.6 0.3 convolution_negate_fusion
  521.0 1.0 fusion.24
  522.0 11.0 %convolution_subtract_fusion = f32[2048,1024]{1,0:T(8,128)} fusion(f32[2048,1024]{1,0:T(8,128)} %param.11, f32[2048,256]{1,0:T(8,128)S(1)} %copy-done.6, f32[256,1024]{1,0:T(8,128)S(1)} %fusion.24), kind=kOutput, calls=%fused_computation.6 | convolution fusion | flops 6444548096 | bytes 19922944 | tf_op jit(solution)/shard_map/dot_general | solution.py:28
  533.0 33.2 %convolution_add_fusion = f32[2048,4096]{1,0:T(8,128)} fusion(f32[2048,4096]{1,0:T(8,128)} %convolution_add_fusion.1, f32[4096,128]{1,0:T(8,128)S(1)} %copy-done.3, f32[4096,128]{1,0:T(8,128)S(1)} %fusion, f32[2048,128]{1,0:T(8,128)S(1)} %fusion.10, f32[2048,128]{1,0:T(8,128)S(1)} %copy-done), kind=kOutput, calls=%fused_computation | convolution fusion | flops 25779765248 | bytes 73400320 | tf_op jit(solution)/shard_map/dot_general | solution.py:53
  (42 shorter events, 0.6 us)
Async XLA Ops:
  7.2 138.5 %all-gather.2.cloned.1.call-start = ((), (), s32[]{:S(2)}) async-start(), calls=%async_computation | async-start | bytes 9437184 | tf_op jit(solution)/shard_map/all_gather | solution.py:81
  7.9 24.7 %copy-start.1 = (f32[2048,128]{1,0:T(8,128)S(1)}, f32[2048,128]{1,0:T(8,128)}, u32[]{:S(2)}) copy-start(f32[2048,128]{1,0:T(8,128)} %param.7) | copy-start | bytes 3145732
  7.9 238.0 %all-reduce.8.cloned.1.call-start = ((), (), s32[]{:S(2)}) async-start(), calls=%async_computation.1 | async-start | bytes 2097152 | tf_op jit(solution)/shard_map/psum | solution.py:43
  8.0 21.9 %collective-permute-start = (f32[2048,128]{1,0:T(8,128)}, f32[2048,128]{1,0:T(8,128)S(1)}, u32[]{:S(2)}, u32[]{:S(2)}) collective-permute-start(f32[2048,128]{1,0:T(8,128)} %param.9), channel_id=1, source_target_pairs={{0,28},{4,0},{8,4},{12,8},{16,12},{20,16},{24,20},{28,24},{1,29},{... | collective-permute-start | bytes 3145736 | tf_op jit(solution)/shard_map/ppermute | solution.py:17
  32.6 1.2 copy-start
  32.6 47.7 %collective-permute-start.1 = (f32[4096,128]{1,0:T(8,128)}, f32[4096,128]{1,0:T(8,128)}, u32[]{:S(2)}, u32[]{:S(2)}) collective-permute-start(f32[4096,128]{1,0:T(8,128)} %pad_maximum_fusion.1), channel_id=1, source_target_pairs={{0,24},{4,28},{8,0},{12,4},{16,8},{20,12},{24,16},{28,20},{1,25},{... | collective-permute-start | bytes 6291464 | tf_op jit(solution)/shard_map/ppermute | solution.py:17
  34.9 12.8 %copy-start.5 = (f32[2048,256]{1,0:T(8,128)}, f32[2048,256]{1,0:T(8,128)S(1)}, u32[]{:S(2)}) copy-start(f32[2048,256]{1,0:T(8,128)S(1)} %get-tuple-element.8) | copy-start | bytes 6291460
  84.1 115.4 %collective-permute-start.2 = (f32[8192,128]{1,0:T(8,128)}, f32[8192,128]{1,0:T(8,128)}, u32[]{:S(2)}, u32[]{:S(2)}) collective-permute-start(f32[8192,128]{1,0:T(8,128)} %pad_maximum_fusion), channel_id=1, source_target_pairs={{0,16},{4,20},{8,24},{12,28},{16,0},{20,4},{24,8},{28,12},{1,17},{... | collective-permute-start | bytes 12582920 | tf_op jit(solution)/shard_map/ppermute | solution.py:17
  191.4 119.4 %all-reduce.14.cloned.1.call-start = ((), (), s32[]{:S(2)}) async-start(), calls=%async_computation.4 | async-start | bytes 4325376 | tf_op jit(solution)/shard_map/psum | solution.py:45
  249.0 190.5 %all-reduce.10.cloned.1.call-start = ((), (), s32[]{:S(2)}) async-start(), calls=%async_computation.2 | async-start | bytes 2097152 | tf_op jit(solution)/shard_map/psum | solution.py:43
  253.5 3.3 copy-start.7
  253.5 3.3 copy-start.9
  310.8 3.6 copy-start.13
  310.8 4.1 copy-start.4
  317.7 33.4 %copy-start.2 = (f32[4096,128]{1,0:T(8,128)S(1)}, f32[4096,128]{1,0:T(8,128)}, u32[]{:S(2)}) copy-start(f32[4096,128]{1,0:T(8,128)} %constant_dynamic-slice_fusion) | copy-start | bytes 6291460
  382.0 131.3 %all-reduce.12.cloned.1.call-start = ((), (), s32[]{:S(2)}) async-start(), calls=%async_computation.3 | async-start | bytes 6553600 | tf_op jit(solution)/shard_map/psum | solution.py:45
  443.1 1.2 copy-start.8
  443.1 1.2 copy-start.10
  513.3 3.6 copy-start.14
  513.3 4.1 copy-start.3
  519.3 1.0 copy-start.12
  519.3 1.6 copy-start.11
  520.3 1.7 copy-start.6
Sparse Core Ops, SparseCore 0:
  9.9 127.2 all-gather.1
  191.5 54.4 all-reduce.7
  249.3 61.4 all-reduce.13
  382.2 51.1 all-reduce.9
  443.3 70.0 all-reduce.11
